TPU v7x, 512 devices: a whole 4x8x8 slice. The times are simulated.
512 devices in a mesh: doc: 32 (over z_hi, y, core), lab: 16 (over z_lo, x).
Axes of the slice: x: 4, y: 8, z: 8 (z_hi: 2, z_lo: 4; z = z_hi * 4 + z_lo), core: 2. Of those that a mesh axis runs over, the one named last changes fastest.
Arguments:
- embeddings: bfloat16 [262144, 768], P(('doc', 'lab')), may hold values from -6 to 6
- positives: int32 [262144, 16], P(('doc', 'lab')), may hold values from 0 to 16383, as said below
- weights: float32 [131072, 768], P(('doc', 'lab')), may hold values from -6 to 6
- parents: int32 [131072], replicated, may hold values from 0 to 254, as said below
- owners: int32 [4, 32], replicated, may hold values from 0 to 15
- shortlist: int32 [4, 512, 4], replicated, may hold values from 0 to 3, as said below
- counts: int32 [4, 512], replicated, may hold values from 1 to 4, as said below
Outputs:
- trained: float32 [131072, 768], P(('doc', 'lab'))
- momentum: float32 [131072, 768], P(('doc', 'lab'))
Inputs may be any that keep to these rules, and one draw needn't show every extreme that they name: `positives`: each positive code is (s * 16 + j) * 256 + l with s < 4, j < 16, l < 256; repeats allowed. parents[l] is a row of l's own block below l's row; row 0 of a block is its own parent. `shortlist`: the 4 tile numbers of one step and block are distinct. `counts`: in every step some block has all 4 slots live.
All inputs are finite; a program needn't handle non-finite values.
Results may differ from a plain program's by a relative error of at most 0.0003.
Values may be sent and summed in bfloat16 or wider, within the bound.
A program may use at most 64 MiB of HBM per device.

v0:
```python
import jax
import jax.numpy as jnp
from jax import lax
from jax.sharding import PartitionSpec as P

TILE = 128
STEPS = 4


learning_rate = 0.1
beta_rate = 0.9
pull_rate = 1.0


def from_root(value, axis, source):
    kept = jnp.where(lax.axis_index(axis) == source, value, 0).astype(value.dtype)
    return lax.psum(kept, axis)


def from_behind(value, axis, by):
    length = lax.axis_size(axis)
    return lax.ppermute(value, axis, [(i, (i + by) % length) for i in range(length)])


def pick_rows(panel, labels, tiles, tile_rows):
    width = panel.shape[1]
    shaped = panel.reshape(panel.shape[0] // tile_rows, tile_rows, width)
    lshaped = labels.reshape(labels.shape[0] // tile_rows, tile_rows, labels.shape[1])
    rows = jnp.take(shaped, tiles, axis=0).reshape(tiles.shape[0] * tile_rows, width)
    picked = jnp.take(lshaped, tiles, axis=0).reshape(tiles.shape[0] * tile_rows, labels.shape[1])
    return (rows, picked)


def block_update(weight, moment, rows, picked, base, parent_rows, live):
    scale = 1.0 / jnp.sqrt(jnp.float32(rows.shape[1]))
    rows32 = rows.astype(jnp.float32)
    scores = (
        jnp.dot(
            rows32, weight.T, precision=lax.Precision.HIGHEST, preferred_element_type=jnp.float32
        )
        * scale
    )
    label_ids = base + jnp.arange(weight.shape[0], dtype=jnp.int32)
    target = jnp.any(picked[:, :, None] == label_ids[None, None, :], axis=1).astype(jnp.float32)
    resid = (jax.nn.sigmoid(scores) - target) * live[:, None]
    grad = (
        jnp.dot(
            resid.T, rows32, precision=lax.Precision.HIGHEST, preferred_element_type=jnp.float32
        )
        * scale
    )
    grad = grad + pull_rate * (weight - jnp.take(weight, parent_rows, axis=0))
    moment = beta_rate * moment + grad
    return (weight - learning_rate * moment, moment)


def local(embeddings, positives, weights, parents, owners, shortlist, counts):
    doc_index = lax.axis_index("doc")
    lab_index = lax.axis_index("lab")
    doc_count = lax.axis_size("doc")
    lab_count = lax.axis_size("lab")
    block_rows = weights.shape[0]
    tile_rows = TILE
    slots = shortlist.shape[2]
    slot_of_row = jnp.arange(slots * tile_rows, dtype=jnp.int32) // tile_rows
    weight = weights
    moment = jnp.zeros_like(weights)
    for step in range(STEPS):
        root = owners[step, doc_index]
        panel = from_root(embeddings, "lab", root)
        labels = from_root(positives, "lab", root)
        met_block = (doc_index - step) % doc_count * lab_count + lab_index
        if step > 0:
            weight, moment = from_behind((weight, moment), "doc", 1)
        tiles = lax.dynamic_index_in_dim(shortlist[step], met_block, 0, keepdims=False)
        rows, picked = pick_rows(panel, labels, tiles, tile_rows)
        live = (slot_of_row < counts[step, met_block]).astype(jnp.float32)
        parent_rows = lax.dynamic_slice_in_dim(parents, met_block * block_rows, block_rows, 0)
        code_base = (step * lab_count + lab_index) * block_rows
        weight, moment = block_update(weight, moment, rows, picked, code_base, parent_rows, live)
    weight, moment = from_behind((weight, moment), "doc", -(STEPS - 1))
    return (weight, moment)


def solution(mesh):
    return jax.shard_map(
        local,
        mesh=mesh,
        in_specs=(
            P(("doc", "lab"), None),
            P(("doc", "lab"), None),
            P(("doc", "lab"), None),
            P(),
            P(),
            P(),
            P(),
        ),
        out_specs=(P(("doc", "lab"), None), P(("doc", "lab"), None)),
        check_vma=False,
    )
```

profile of v0, /device:TPU:55, one launch (start us, length us, event | category | flops | bytes accessed | tf_op | source)
XLA Modules:
  0.0 590.3 jit_solution(14270951001734933305)
XLA Ops:
  7.2 1.5 constant_dynamic-slice_fusion.5
  13.4 2.9 broadcast_select_fusion.4
  18.2 1.1 gather_fusion.2
  19.7 1.5 constant_dynamic-slice_fusion.4
  23.9 144.6 %all-reduce.5.cloned.1.call-done = (s32[4,128,16]{1,2,0:T(8,128)}, s32[4,128,16]{1,2,0:T(8,128)}, s32[4,128,16]{1,2,0:T(8,128)}, s32[4,128,16]{1,2,0:T(8,128)}) async-done(((s32[4,128,16]{1,2,0:T(8,128)}, s32[4,128,16]{1,2,0:T(8,128)}, s32[4,128,16]{1,2,0:T(8,128)}, s32[4,128,16]{1,2,0:T(8,128)}), (s32[4,128,16]{1,2,0:T(8,128)}, s32[4,128,16]{1,2,0:T(8,128)}, s32[4,128,16]{1,2,0:T(8,128)}, ...) | async-done | bytes 131088 | tf_op jit(solution)/shard_map/psum | solution.py:17
  168.5 1.3 gather_fusion.1
  170.1 5.9 compare_reduce_fusion.3
  175.9 175.2 %all-reduce.7.cloned.1.call-done = (bf16[4,128,768]{2,1,0:T(8,128)(2,1)}, bf16[4,128,768]{2,1,0:T(8,128)(2,1)}, bf16[4,128,768]{2,1,0:T(8,128)(2,1)}, bf16[4,128,768]{2,1,0:T(8,128)(2,1)}) async-done(((bf16[4,128,768]{2,1,0:T(8,128)(2,1)}, bf16[4,128,768]{2,1,0:T(8,128)(2,1)}, bf16[4,128,768]{2,1,0:T(8,128)(2,1)}, bf16[4,128,768]{2,1,0:T(8,128)(2,1)}), (bf16[4,128,768]{2,1,0:T(8,128)(2,1)}, ...) | async-done | bytes 3145744 | tf_op jit(solution)/shard_map/psum | solution.py:17
  351.1 1.7 gather_fusion
  354.0 1.8 multiply_subtract_fusion.3
  355.8 12.5 %collective-permute-start = (f32[256,768]{1,0:T(8,128)}, f32[256,768]{1,0:T(8,128)S(1)}, u32[]{:S(2)}, u32[]{:S(2)}) collective-permute-start(f32[256,768]{1,0:T(8,128)} %get-tuple-element.53), channel_id=1, source_target_pairs={{0,16},{16,32},{32,48},{48,64},{64,80},{80,96},{96,112},{112,128},... | collective-permute-start | bytes 2359304 | tf_op jit(solution)/shard_map/ppermute | solution.py:22
  369.1 5.9 compare_reduce_fusion.2
  375.0 1.7 gather_fusion.3
  376.8 1.9 collective-permute-start.1
  378.9 1.1 gather_fusion.5
  381.8 5.8 collective-permute-done.1
  387.6 2.3 multiply_subtract_fusion.2
  389.9 4.6 collective-permute-start.2
  395.4 5.9 compare_reduce_fusion.1
  401.9 15.6 %collective-permute-start.3 = (f32[256,768]{1,0:T(8,128)S(1)}, f32[256,768]{1,0:T(8,128)}, u32[]{:S(2)}, u32[]{:S(2)}) collective-permute-start(f32[256,768]{1,0:T(8,128)S(1)} %get-tuple-element.22), channel_id=1, source_target_pairs={{0,16},{16,32},{32,48},{48,64},{64,80},{80,96},{96,112},{112,128},... | collective-permute-start | bytes 2359304 | tf_op jit(solution)/shard_map/ppermute | solution.py:22
  417.6 1.1 gather_fusion.8
  420.6 5.6 collective-permute-done.3
  426.2 2.3 multiply_subtract_fusion.1
  428.5 7.3 %collective-permute-start.4 = (f32[256,768]{1,0:T(8,128)}, f32[256,768]{1,0:T(8,128)S(1)}, u32[]{:S(2)}, u32[]{:S(2)}) collective-permute-start(f32[256,768]{1,0:T(8,128)} %get-tuple-element.17), channel_id=1, source_target_pairs={{0,16},{16,32},{32,48},{48,64},{64,80},{80,96},{96,112},{112,128},... | collective-permute-start | bytes 2359304 | tf_op jit(solution)/shard_map/ppermute | solution.py:22
  436.7 5.9 compare_reduce_fusion
  443.2 22.2 %collective-permute-start.5 = (f32[256,768]{1,0:T(8,128)S(1)}, f32[256,768]{1,0:T(8,128)}, u32[]{:S(2)}, u32[]{:S(2)}) collective-permute-start(f32[256,768]{1,0:T(8,128)S(1)} %get-tuple-element.18), channel_id=1, source_target_pairs={{0,16},{16,32},{32,48},{48,64},{64,80},{80,96},{96,112},{112,128},... | collective-permute-start | bytes 2359304 | tf_op jit(solution)/shard_map/ppermute | solution.py:22
  468.5 5.8 collective-permute-done.5
  474.3 1.4 multiply_subtract_fusion
  475.8 1.9 collective-permute-start.6
  477.7 1.9 collective-permute-start.7
  479.6 87.9 %collective-permute-done.6 = f32[256,768]{1,0:T(8,128)S(1)} collective-permute-done((f32[256,768]{1,0:T(8,128)S(1)}, f32[256,768]{1,0:T(8,128)S(1)}, u32[]{:S(2)}, u32[]{:S(2)}) %collective-permute-start.6) | collective-permute-done | bytes 786464 | tf_op jit(solution)/shard_map/ppermute | solution.py:22
  567.5 14.3 %collective-permute-done.7 = f32[256,768]{1,0:T(8,128)S(1)} collective-permute-done((f32[256,768]{1,0:T(8,128)S(1)}, f32[256,768]{1,0:T(8,128)S(1)}, u32[]{:S(2)}, u32[]{:S(2)}) %collective-permute-start.7) | collective-permute-done | bytes 786464 | tf_op jit(solution)/shard_map/ppermute | solution.py:22
  (77 shorter events, 20.4 us)
Async XLA Ops:
  7.2 161.4 %all-reduce.5.cloned.1.call-start = ((), (), s32[]{:S(2)}) async-start(), calls=%async_computation | async-start | bytes 262144 | tf_op jit(solution)/shard_map/psum | solution.py:17
  13.3 337.8 %all-reduce.7.cloned.1.call-start = ((), (), s32[]{:S(2)}) async-start(), calls=%async_computation.1 | async-start | bytes 6291456 | tf_op jit(solution)/shard_map/psum | solution.py:17
  16.2 0.8 copy-start.6
  16.2 2.0 copy-start
  354.0 14.4 %copy-start.3 = (s32[4,128,16]{1,2,0:T(8,128)S(1)}, s32[4,128,16]{1,2,0:T(8,128)}, u32[]{:S(2)}) copy-start(s32[4,128,16]{1,2,0:T(8,128)} %get-tuple-element.6) | copy-start | bytes 98308
  355.8 23.0 %collective-permute-start = (f32[256,768]{1,0:T(8,128)}, f32[256,768]{1,0:T(8,128)S(1)}, u32[]{:S(2)}, u32[]{:S(2)}) collective-permute-start(f32[256,768]{1,0:T(8,128)} %get-tuple-element.53), channel_id=1, source_target_pairs={{0,16},{16,32},{32,48},{48,64},{64,80},{80,96},{96,112},{112,128},... | collective-permute-start | bytes 2359304 | tf_op jit(solution)/shard_map/ppermute | solution.py:22
  376.8 10.8 %collective-permute-start.1 = (f32[256,768]{1,0:T(8,128)S(1)}, f32[256,768]{1,0:T(8,128)}, u32[]{:S(2)}, u32[]{:S(2)}) collective-permute-start(f32[256,768]{1,0:T(8,128)S(1)} %get-tuple-element.54), channel_id=1, source_target_pairs={{0,16},{16,32},{32,48},{48,64},{64,80},{80,96},{96,112},{112,128},... | collective-permute-start | bytes 2359304 | tf_op jit(solution)/shard_map/ppermute | solution.py:22
  387.6 7.0 %copy-start.2 = (s32[4,128,16]{1,2,0:T(8,128)S(1)}, s32[4,128,16]{1,2,0:T(8,128)}, u32[]{:S(2)}) copy-start(s32[4,128,16]{1,2,0:T(8,128)} %get-tuple-element.7) | copy-start | bytes 98308
  389.9 11.3 %copy-start.5 = (bf16[4,128,768]{2,1,0:T(8,128)(2,1)S(1)}, bf16[4,128,768]{2,1,0:T(8,128)(2,1)}, u32[]{:S(2)}) copy-start(bf16[4,128,768]{2,1,0:T(8,128)(2,1)} %get-tuple-element.11) | copy-start | bytes 2359300
  389.9 27.7 %collective-permute-start.2 = (f32[256,768]{1,0:T(8,128)}, f32[256,768]{1,0:T(8,128)S(1)}, u32[]{:S(2)}, u32[]{:S(2)}) collective-permute-start(f32[256,768]{1,0:T(8,128)} %get-tuple-element.21), channel_id=1, source_target_pairs={{0,16},{16,32},{32,48},{48,64},{64,80},{80,96},{96,112},{112,128},... | collective-permute-start | bytes 2359304 | tf_op jit(solution)/shard_map/ppermute | solution.py:22
  401.9 24.3 %collective-permute-start.3 = (f32[256,768]{1,0:T(8,128)S(1)}, f32[256,768]{1,0:T(8,128)}, u32[]{:S(2)}, u32[]{:S(2)}) collective-permute-start(f32[256,768]{1,0:T(8,128)S(1)} %get-tuple-element.22), channel_id=1, source_target_pairs={{0,16},{16,32},{32,48},{48,64},{64,80},{80,96},{96,112},{112,128},... | collective-permute-start | bytes 2359304 | tf_op jit(solution)/shard_map/ppermute | solution.py:22
  426.2 9.7 %copy-start.1 = (s32[4,128,16]{1,2,0:T(8,128)S(1)}, s32[4,128,16]{1,2,0:T(8,128)}, u32[]{:S(2)}) copy-start(s32[4,128,16]{1,2,0:T(8,128)} %get-tuple-element.8) | copy-start | bytes 98308
  428.5 14.0 %copy-start.4 = (bf16[4,128,768]{2,1,0:T(8,128)(2,1)S(1)}, bf16[4,128,768]{2,1,0:T(8,128)(2,1)}, u32[]{:S(2)}) copy-start(bf16[4,128,768]{2,1,0:T(8,128)(2,1)} %get-tuple-element.12) | copy-start | bytes 2359300
  428.5 37.0 %collective-permute-start.4 = (f32[256,768]{1,0:T(8,128)}, f32[256,768]{1,0:T(8,128)S(1)}, u32[]{:S(2)}, u32[]{:S(2)}) collective-permute-start(f32[256,768]{1,0:T(8,128)} %get-tuple-element.17), channel_id=1, source_target_pairs={{0,16},{16,32},{32,48},{48,64},{64,80},{80,96},{96,112},{112,128},... | collective-permute-start | bytes 2359304 | tf_op jit(solution)/shard_map/ppermute | solution.py:22
  443.2 31.1 %collective-permute-start.5 = (f32[256,768]{1,0:T(8,128)S(1)}, f32[256,768]{1,0:T(8,128)}, u32[]{:S(2)}, u32[]{:S(2)}) collective-permute-start(f32[256,768]{1,0:T(8,128)S(1)} %get-tuple-element.18), channel_id=1, source_target_pairs={{0,16},{16,32},{32,48},{48,64},{64,80},{80,96},{96,112},{112,128},... | collective-permute-start | bytes 2359304 | tf_op jit(solution)/shard_map/ppermute | solution.py:22
  475.8 91.7 %collective-permute-start.6 = (f32[256,768]{1,0:T(8,128)S(1)}, f32[256,768]{1,0:T(8,128)S(1)}, u32[]{:S(2)}, u32[]{:S(2)}) collective-permute-start(f32[256,768]{1,0:T(8,128)S(1)} %get-tuple-element.13), channel_id=1, source_target_pairs={{0,464},{16,480},{32,496},{48,0},{64,16},{80,32},{96,48},{112,64},... | collective-permute-start | bytes 2359304 | tf_op jit(solution)/shard_map/ppermute | solution.py:22
  477.7 104.1 %collective-permute-start.7 = (f32[256,768]{1,0:T(8,128)S(1)}, f32[256,768]{1,0:T(8,128)S(1)}, u32[]{:S(2)}, u32[]{:S(2)}) collective-permute-start(f32[256,768]{1,0:T(8,128)S(1)} %get-tuple-element.14), channel_id=1, source_target_pairs={{0,464},{16,480},{32,496},{48,0},{64,16},{80,32},{96,48},{112,64},... | collective-permute-start | bytes 2359304 | tf_op jit(solution)/shard_map/ppermute | solution.py:22
Sparse Core Ops, SparseCore 0:
  13.4 155.0 all-reduce.4
  172.6 178.4 all-reduce.6
where the time goes:
time: 591 us; the launch traced here: 590 us
  waiting for transfers between devices  439 us (74%)
  starting transfers between devices  68.1 us (12%)
  other arithmetic  37.6 us (6%)
  local copies, waits for them, and re-layouts  19.8 us (3%)
  between operations  17.3 us (3%)
  matrix products  8.22 us (1%)
    psum x2, waiting for transfers between devices, from_root(): return lax.psum(kept, axis)  320 us
    ppermute x8, waiting for transfers between devices, from_behind(): lax.ppermute(value, axis, [(i, (i + by) % length) for i in range(length)])  119 us
    ppermute x8, starting transfers between devices, from_behind(): lax.ppermute(value, axis, [(i, (i + by) % length) for i in range(length)])  68 us
    reduce_or x4, other arithmetic, block_update(): jnp.any(picked[:, :, None] == label_ids[None, None, :], axis=1)  23.6 us
  transfers between devices with their start and end apart: 10, of which 7 were waited for; matrix products, arithmetic and copies ran while one was open for 8% of the time, Pallas kernels for 0%

commit v1 on v0

v1 whole, which is shorter than its diff:
```python
import functools

import jax
import jax.numpy as jnp
from jax import lax
from jax.experimental import pallas as pl
from jax.experimental.pallas import tpu as pltpu
from jax.sharding import PartitionSpec as P

MESH = pl.DeviceIdType.MESH

TILE = 128
STEPS = 4
RING = 4

learning_rate = 0.1
beta_rate = 0.9
pull_rate = 1.0


def split(value):
    high = value.astype(jnp.bfloat16)
    low = (value - high.astype(jnp.float32)).astype(jnp.bfloat16)
    return high, low


def train_kernel(
    doc_count,
    owners,
    counts,
    shortlist,
    parents,
    embeddings,
    positives,
    weights,
    trained,
    momentum,
    emb,
    pos,
    par,
    pull,
    src,
    row,
    shift,
    cand,
    inward,
    outward,
    arrived,
    panel,
    load_sem,
    row_send,
    row_recv,
    shift_send,
    shift_recv,
    in_send,
    out_send,
    line_recv,
    ring_send,
    ring_recv,
    pass_send,
    pass_recv,
):
    doc = lax.axis_index("doc")
    lab = lax.axis_index("lab")
    z, x = lab // RING, lab % RING
    block = doc * (RING * RING) + lab
    width = embeddings.shape[1]
    lanes = width // TILE
    code_rows = lanes * TILE
    tile_rows = src.shape[1]
    half = tile_rows // 2
    picks = positives.shape[0]
    labels = weights.shape[0]
    scale = 1.0 / (float(width) ** 0.5)

    def at_x(k):
        return (doc, z * RING + (x + k) % RING)

    def at_z(to):
        return (doc, to * RING + x)

    def at_doc(k):
        return ((doc + k) % doc_count, lab)

    low_half = z < RING // 2
    side = jnp.where(low_half, 0, 1)
    far = jnp.where(low_half, z + 1, z - 1)
    near = jnp.where(low_half, z - 1, z + 1)
    has_near = (z % (RING - 1)) != 0

    loads = [
        pltpu.make_async_copy(embeddings, emb, load_sem.at[0]),
        pltpu.make_async_copy(positives, pos, load_sem.at[1]),
        pltpu.make_async_copy(weights, trained, load_sem.at[2]),
        pltpu.make_async_copy(parents.at[pl.ds(8 * (block // 4), 8)], par, load_sem.at[3]),
    ]
    for load in loads:
        load.start()

    barrier = pltpu.get_barrier_semaphore()
    partners = [at_x(k) for k in range(1, RING)]
    for k in range(1, STEPS):
        partners += [at_doc(k), at_doc(-k)]
    partners.append(at_z(far))
    for partner in partners:
        pl.semaphore_signal(barrier, inc=1, device_id=partner, device_id_type=MESH)

    @pl.when(has_near)
    def _():
        pl.semaphore_signal(barrier, inc=1, device_id=at_z(near), device_id_type=MESH)

    loads[0].wait()
    loads[1].wait()
    for t in range(RING):
        for c in range(lanes):
            src[t, pl.ds(c * TILE, TILE), :] = emb[pl.ds(t * TILE, TILE), pl.ds(c * TILE, TILE)]
        code = pos[:, pl.ds(t * TILE, TILE)]
        src[t, pl.ds(code_rows, picks), :] = (code // labels).astype(jnp.float32).astype(jnp.bfloat16)
        src[t, pl.ds(code_rows + picks, picks), :] = (code % labels).astype(jnp.float32).astype(jnp.bfloat16)
    row[x] = src[x]

    pl.semaphore_wait(barrier, len(partners) + jnp.where(has_near, 1, 0))

    def remote(source, target, send, recv, device):
        return pltpu.make_async_remote_copy(
            src_ref=source,
            dst_ref=target,
            send_sem=send,
            recv_sem=recv,
            device_id=device,
            device_id_type=MESH,
        )

    row_copies = []
    for k in range(1, RING):
        to = (x + k) % RING
        row_copies.append(
            remote(src.at[to], row.at[x], row_send.at[k - 1], row_recv.at[k - 1], at_x(k))
        )
    for copy in row_copies:
        copy.start()

    loads[3].wait()
    ids = lax.broadcasted_iota(jnp.int32, (labels, TILE), 0)
    columns = []
    for c in range(labels // TILE):
        parent = par[pl.ds((block % 4) * (labels // TILE) + c, 1), :]
        own = lax.broadcasted_iota(jnp.int32, (labels, TILE), 1) + c * TILE
        columns.append(
            (ids == own).astype(jnp.float32) - (ids == parent).astype(jnp.float32)
        )
    pull[...] = jnp.transpose(jnp.concatenate(columns, axis=1)).astype(jnp.bfloat16)
    momentum[...] = jnp.zeros_like(momentum)
    loads[2].wait()

    for copy in row_copies:
        copy.wait_recv()

    shift_copies = {}
    for s in range(1, STEPS):
        shift_copies[s] = remote(
            shift.at[s - 1],
            cand.at[s],
            shift_send.at[s - 1],
            shift_recv.at[s - 1],
            at_doc(-s),
        )

    def choose(s):
        picked = row[owners[s, doc] % RING]
        if s == 0:
            cand[0] = picked
        else:
            shift[s - 1] = picked
            shift_copies[s].start()

    def owner_z(s):
        return owners[s, (doc + s) % doc_count] // RING

    def line_in(s):
        return remote(
            inward.at[s], arrived.at[side, s], in_send.at[s], line_recv.at[side, s], at_z(far)
        )

    def line_out(s):
        return remote(
            outward.at[s],
            arrived.at[1 - side, s],
            out_send.at[s],
            line_recv.at[1 - side, s],
            at_z(near),
        )

    def wait_near(s):
        remote(
            inward.at[s], arrived.at[side, s], in_send.at[s], line_recv.at[side, s], at_z(far)
        ).wait_recv()

    def wait_far(s):
        remote(
            outward.at[s], arrived.at[1 - side, s], out_send.at[s], line_recv.at[1 - side, s], at_z(far)
        ).wait_recv()

    def flow_in(s):
        if s > 0:
            shift_copies[s].wait_recv()

        @pl.when(has_near)
        def _():
            wait_near(s)
            inward[s] = jnp.where(owner_z(s) == z, cand[s], arrived[side, s])

        @pl.when(jnp.logical_not(has_near))
        def _():
            inward[s] = cand[s]

        line_in(s).start()

    def ring_copies(s):
        return (
            remote(panel.at[s, x], panel.at[s, x], ring_send.at[0, s], ring_recv.at[0, s], at_x(1)),
            remote(panel.at[s, x], panel.at[s, x], ring_send.at[1, s], ring_recv.at[1, s], at_x(-1)),
        )

    def pass_copies(s):
        left = (x + RING - 1) % RING
        right = (x + 1) % RING
        first = panel.at[s, left, pl.ds(0, half)]
        second = panel.at[s, right, pl.ds(half, half)]
        return (
            remote(first, first, pass_send.at[0, s], pass_recv.at[0, s], at_x(1)),
            remote(second, second, pass_send.at[1, s], pass_recv.at[1, s], at_x(-1)),
        )

    def flow_out(s):
        wait_far(s)
        mine = owner_z(s) == z

        @pl.when(has_near)
        def _():
            outward[s] = jnp.where(mine, cand[s], arrived[1 - side, s])
            line_out(s).start()
            nearer = jnp.where(low_half, owner_z(s) <= z, owner_z(s) >= z)
            panel[s, x] = jnp.where(nearer, inward[s], arrived[1 - side, s])

        @pl.when(jnp.logical_not(has_near))
        def _():
            panel[s, x] = jnp.where(mine, cand[s], arrived[1 - side, s])

        for copy in ring_copies(s):
            copy.start()

    def ring_pass(s):
        for copy in ring_copies(s):
            copy.wait_recv()
        for copy in pass_copies(s):
            copy.start()

    def tile_rows_of(s, t):
        return jnp.concatenate(
            [panel[s, t, pl.ds(c * TILE, TILE), :] for c in range(lanes)], axis=1
        )

    def update(s):
        for copy in pass_copies(s):
            copy.wait_recv()
        high, low = split(trained[...])
        count = counts[s, block]
        grad = None
        for pair in range(RING // 2):
            tiles = (2 * pair, 2 * pair + 1)
            rows = jnp.concatenate([tile_rows_of(s, t) for t in tiles], axis=0)
            contract = (((1,), (1,)), ((), ()))
            scores = (
                lax.dot_general(high, rows, contract, preferred_element_type=jnp.float32)
                + lax.dot_general(low, rows, contract, preferred_element_type=jnp.float32)
            ) * scale
            keys, lives = [], []
            for t in tiles:
                group = panel[s, t, pl.ds(code_rows, picks), :].astype(jnp.float32)
                label = panel[s, t, pl.ds(code_rows + picks, picks), :].astype(jnp.float32)
                wanted = (s * RING * RING + lab).astype(jnp.float32)
                keys.append(jnp.where(group == wanted, label, -1.0))
                live = jnp.float32(0.0)
                for k in range(RING):
                    met = jnp.logical_and(count > k, shortlist[s, k, block] == t)
                    live = jnp.where(met, jnp.float32(1.0), live)
                lives.append(jnp.full((1, TILE), live, jnp.float32))
            keys = jnp.concatenate(keys, axis=1)
            lives = jnp.concatenate(lives, axis=1)
            names = lax.broadcasted_iota(jnp.int32, scores.shape, 0).astype(jnp.float32)
            hit = names == keys[0:1, :]
            for p in range(1, picks):
                hit = jnp.logical_or(hit, names == keys[p : p + 1, :])
            resid = (jax.nn.sigmoid(scores) - jnp.where(hit, 1.0, 0.0)) * lives
            rhigh, rlow = split(resid)
            part = jnp.dot(rhigh, rows, preferred_element_type=jnp.float32) + jnp.dot(
                rlow, rows, preferred_element_type=jnp.float32
            )
            grad = part if grad is None else grad + part
        pulled = jnp.dot(pull[...], high, preferred_element_type=jnp.float32) + jnp.dot(
            pull[...], low, preferred_element_type=jnp.float32
        )
        moment = beta_rate * momentum[...] + (grad * scale + pull_rate * pulled)
        momentum[...] = moment
        trained[...] = trained[...] - learning_rate * moment

    choose(0)
    flow_in(0)
    for s in range(1, STEPS):
        choose(s)
    flow_in(1)
    flow_out(0)
    flow_in(2)
    flow_out(1)
    ring_pass(0)
    flow_in(3)
    flow_out(2)
    ring_pass(1)
    update(0)
    flow_out(3)
    ring_pass(2)
    update(1)
    ring_pass(3)
    update(2)
    update(3)

    for copy in row_copies:
        copy.wait_send()
    for s in range(1, STEPS):
        shift_copies[s].wait_send()
    for s in range(STEPS):
        line_in(s).wait_send()

        @pl.when(has_near)
        def _():
            line_out(s).wait_send()

        for copy in ring_copies(s) + pass_copies(s):
            copy.wait_send()


def local(doc_count, embeddings, positives, weights, parents, owners, shortlist, counts):
    rows, width = embeddings.shape
    labels = weights.shape[0]
    picks = positives.shape[1]
    tile_rows = width + 2 * picks
    tile = (tile_rows, TILE)
    half = jnp.bfloat16
    dma = pltpu.SemaphoreType.DMA
    out = jax.ShapeDtypeStruct(weights.shape, jnp.float32)
    smem = pl.BlockSpec(memory_space=pltpu.SMEM)
    hbm = pl.BlockSpec(memory_space=pl.ANY)
    vmem = pl.BlockSpec(memory_space=pltpu.VMEM)
    return pl.pallas_call(
        functools.partial(train_kernel, doc_count),
        out_shape=(out, out),
        in_specs=[smem, smem, smem, hbm, hbm, hbm, hbm],
        out_specs=(vmem, vmem),
        scratch_shapes=[
            pltpu.VMEM((rows, width), half),
            pltpu.VMEM((picks, rows), jnp.int32),
            pltpu.VMEM((8, TILE), jnp.int32),
            pltpu.VMEM((labels, labels), half),
            pltpu.VMEM((RING,) + tile, half),
            pltpu.VMEM((RING,) + tile, half),
            pltpu.VMEM((STEPS - 1,) + tile, half),
            pltpu.VMEM((STEPS,) + tile, half),
            pltpu.VMEM((STEPS,) + tile, half),
            pltpu.VMEM((STEPS,) + tile, half),
            pltpu.VMEM((2, STEPS) + tile, half),
            pltpu.VMEM((STEPS, RING) + tile, half),
            dma((4,)),
            dma((RING - 1,)),
            dma((RING - 1,)),
            dma((STEPS - 1,)),
            dma((STEPS - 1,)),
            dma((STEPS,)),
            dma((STEPS,)),
            dma((2, STEPS)),
            dma((2, STEPS)),
            dma((2, STEPS)),
            dma((2, STEPS)),
            dma((2, STEPS)),
        ],
        compiler_params=pltpu.CompilerParams(
            collective_id=0, has_side_effects=True, vmem_limit_bytes=48 * 1024 * 1024
        ),
    )(
        owners,
        counts,
        jnp.transpose(shortlist, (0, 2, 1)),
        parents.reshape(-1, TILE),
        embeddings,
        positives.T,
        weights,
    )


def solution(mesh):
    return jax.shard_map(
        functools.partial(local, mesh.shape["doc"]),
        mesh=mesh,
        in_specs=(
            P(("doc", "lab"), None),
            P(("doc", "lab"), None),
            P(("doc", "lab"), None),
            P(),
            P(),
            P(),
            P(),
        ),
        out_specs=(P(("doc", "lab"), None), P(("doc", "lab"), None)),
        check_vma=False,
    )
```

time: 591 us -> 114 us (0.19)
  the two profiles are of different devices: /device:TPU:55 before, /device:TPU:56 now
where the time goes in v1:
time: 114 us
  Pallas kernels  105 us (92%)
  local copies, waits for them, and re-layouts  7.95 us (7%)
    pallas_call x1, Pallas kernels, local(): pl.pallas_call(functools.partial(train_kernel, doc_count), out_shape=(out...  105 us
    unnamed x16, local copies, waits for them, and re-layouts  7.95 us

profile of v1, /device:TPU:56, one launch (start us, length us, event | category | flops | bytes accessed | tf_op | source)
XLA Modules:
  0.0 113.9 jit_solution(8957108294857743059)
XLA Ops:
  0.6 0.0 copy-start.6
  0.6 0.7 copy-done.6
  1.3 0.0 copy-start
  1.3 1.1 copy-done
  2.4 0.0 copy-start.1
  2.5 1.1 copy-done.1
  3.6 0.0 copy-start.2
  3.6 1.0 copy-done.2
  4.6 0.0 copy-start.3
  4.6 0.8 copy-done.3
  5.4 0.0 copy-start.4
  5.4 0.8 copy-done.4
  6.1 0.0 copy-start.5
  6.1 0.7 copy-done.5
  6.8 105.3 %shard_map.86 = (f32[256,768]{1,0:T(8,128)S(1)}, f32[256,768]{1,0:T(8,128)S(1)}) custom-call(s32[4,32]{1,0:T(4,128)S(1)} %copy-done.6, s32[4,512]{1,0:T(4,128)S(1)} %copy-done.5, s32[4,4,512]{2,1,0:T(4,128)S(1)} %bitcast.4, s32[1024,128]{1,0:T(8,128)S(1)} %bitcast.3, bf16[512,768]{1,0:T(8,128)(2,1)S(1)} %copy-done, s32[16,512]{1,0:T(8,128)S(1)} %bitcast.5, ...), custom_call_target="tpu_custom_call" | custom-call | tf_op jit(solution)/shard_map/pallas_call | solution.py:355
  112.1 0.9 copy.11
  113.0 0.9 copy.12
Async XLA Ops:
  0.6 0.7 copy-start.6
  1.3 1.1 copy-start
  2.4 1.1 copy-start.1
  3.6 1.0 copy-start.2
  4.6 0.8 copy-start.3
  5.4 0.8 copy-start.4
  6.1 0.7 copy-start.5

commit v2 on v1

v2 whole, which is shorter than its diff:
```python
import functools

import jax
import jax.numpy as jnp
from jax import lax
from jax.experimental import pallas as pl
from jax.experimental.pallas import tpu as pltpu
from jax.sharding import PartitionSpec as P

MESH = pl.DeviceIdType.MESH

TILE = 128
STEPS = 4
RING = 4
PARTS = 2

learning_rate = 0.1
beta_rate = 0.9
pull_rate = 1.0


def split(value):
    high = value.astype(jnp.bfloat16)
    low = (value - high.astype(jnp.float32)).astype(jnp.bfloat16)
    return high, low


def train_kernel(
    doc_count,
    owners_all,
    counts_all,
    shortlist_all,
    parents,
    embeddings,
    positives,
    weights,
    trained,
    momentum,
    owners,
    counts,
    shortlist,
    emb,
    pos,
    par,
    pull,
    src,
    row_first,
    row_second,
    cand,
    inward,
    outward,
    arrived,
    ready,
    panel,
    load_sem,
    row_send,
    row_recv,
    in_send,
    out_send,
    line_recv,
    shift_send,
    shift_recv,
    spread_send,
    ring_send,
    ring_recv,
    pass_send,
    pass_recv,
):
    doc = lax.axis_index("doc")
    lab = lax.axis_index("lab")
    z, x = lab // RING, lab % RING
    block = doc * (RING * RING) + lab
    width = embeddings.shape[1]
    lanes = width // TILE
    code_rows = lanes * TILE
    part_rows = src.shape[1] // PARTS
    picks = positives.shape[0]
    labels = weights.shape[0]
    scale = 1.0 / (float(width) ** 0.5)
    row = (row_first, row_second)
    span = doc_count // 2
    place = doc % span

    def at_x(k):
        return (doc, z * RING + (x + k) % RING)

    def at_z(to):
        return (doc, to * RING + x)

    def across(k, crosses):
        to_z = jnp.where(crosses, RING - 1 - z, z)
        return ((doc + k) % doc_count, to_z * RING + x)

    sends_over = [place < s for s in range(STEPS)]
    takes_over = [place + s >= span for s in range(STEPS)]

    low_half = z < RING // 2
    side = jnp.where(low_half, 0, 1)
    far = jnp.where(low_half, z + 1, z - 1)
    near = jnp.where(low_half, z - 1, z + 1)
    has_near = (z % (RING - 1)) != 0

    lane_block = pl.ds(TILE * (block // TILE), TILE)
    loads = [
        pltpu.make_async_copy(embeddings, emb, load_sem.at[0]),
        pltpu.make_async_copy(positives, pos, load_sem.at[1]),
        pltpu.make_async_copy(owners_all, owners, load_sem.at[2]),
        pltpu.make_async_copy(counts_all.at[:, lane_block], counts, load_sem.at[3]),
        pltpu.make_async_copy(shortlist_all.at[:, :, lane_block], shortlist, load_sem.at[4]),
        pltpu.make_async_copy(parents.at[pl.ds(8 * (block // 4), 8)], par, load_sem.at[5]),
        pltpu.make_async_copy(weights, trained, load_sem.at[6]),
    ]
    for load in loads:
        load.start()

    barrier = pltpu.get_barrier_semaphore()
    partners = [at_x(k) for k in range(1, RING)]
    for s in range(1, STEPS):
        partners += [across(-s, sends_over[s]), across(s, takes_over[s])]
    partners.append(at_z(far))
    for partner in partners:
        pl.semaphore_signal(barrier, inc=1, device_id=partner, device_id_type=MESH)

    @pl.when(has_near)
    def _():
        pl.semaphore_signal(barrier, inc=1, device_id=at_z(near), device_id_type=MESH)

    loads[0].wait()
    loads[1].wait()
    for t in range(RING):
        for c in range(lanes):
            src[t, pl.ds(c * TILE, TILE), :] = emb[pl.ds(t * TILE, TILE), pl.ds(c * TILE, TILE)]
        code = pos[:, pl.ds(t * TILE, TILE)]
        src[t, pl.ds(code_rows, picks), :] = (code // labels).astype(jnp.float32).astype(jnp.bfloat16)
        src[t, pl.ds(code_rows + picks, picks), :] = (code % labels).astype(jnp.float32).astype(jnp.bfloat16)
    for h in range(PARTS):
        row[h][x] = src[x, pl.ds(h * part_rows, part_rows), :]

    pl.semaphore_wait(barrier, len(partners) + jnp.where(has_near, 1, 0))

    def remote(source, target, send, recv, device):
        return pltpu.make_async_remote_copy(
            src_ref=source,
            dst_ref=target,
            send_sem=send,
            recv_sem=recv,
            device_id=device,
            device_id_type=MESH,
        )

    parts = [pl.ds(h * part_rows, part_rows) for h in range(PARTS)]

    def row_copies(h):
        return [
            remote(
                src.at[(x + k) % RING, parts[h]],
                row[h].at[x],
                row_send.at[h, k - 1],
                row_recv.at[h, k - 1],
                at_x(k),
            )
            for k in range(1, RING)
        ]

    def row_start(h):
        for copy in row_copies(h):
            copy.start()

    def row_wait(h):
        for copy in row_copies(h):
            copy.wait_recv()

    def owner_z(s, home):
        return owners[s, home] // RING

    def line_in(h, s):
        return remote(
            inward.at[s, parts[h]],
            arrived.at[side, s, parts[h]],
            in_send.at[h, s],
            line_recv.at[side, h, s],
            at_z(far),
        )

    def line_out(h, s, to):
        return remote(
            outward.at[s, parts[h]],
            arrived.at[1 - side, s, parts[h]],
            out_send.at[h, s],
            line_recv.at[1 - side, h, s],
            at_z(to),
        )

    def goes_in(h, s):
        return jnp.logical_or(jnp.logical_not(sends_over[s]), side == h)

    def goes_out(h, s):
        return jnp.logical_or(jnp.logical_not(sends_over[s]), side != h)

    def over_copy(h, s):
        target = panel.at[s, x, parts[h]]
        return remote(
            outward.at[s, parts[h]], target, shift_send.at[h, s], shift_recv.at[h, s], across(-s, True)
        )

    def shift_copy(h, s):
        target = panel.at[s, x, parts[h]]
        return remote(
            ready.at[s, parts[h]], target, shift_send.at[h, s], shift_recv.at[h, s], across(-s, False)
        )

    def flow_in(h, s):
        cand[s, parts[h], :] = row[h][owners[s, doc] % RING]

        @pl.when(goes_in(h, s))
        def _():
            @pl.when(has_near)
            def _():
                line_in(h, s).wait_recv()
                inward[s, parts[h], :] = jnp.where(
                    owner_z(s, doc) == z, cand[s, parts[h], :], arrived[side, s, parts[h], :]
                )

            @pl.when(jnp.logical_not(has_near))
            def _():
                inward[s, parts[h], :] = cand[s, parts[h], :]

            line_in(h, s).start()

    def flow_out(h, s):
        mine = owner_z(s, doc) == z

        @pl.when(goes_out(h, s))
        def _():
            line_out(h, s, far).wait_recv()
            outward[s, parts[h], :] = jnp.where(
                mine, cand[s, parts[h], :], arrived[1 - side, s, parts[h], :]
            )

            @pl.when(has_near)
            def _():
                line_out(h, s, near).start()

        over = jnp.logical_and(sends_over[s], side != h)

        @pl.when(jnp.logical_and(over, jnp.logical_not(has_near)))
        def _():
            over_copy(h, s).start()

        @pl.when(jnp.logical_not(sends_over[s]))
        def _():
            nearer = jnp.where(low_half, owner_z(s, doc) <= z, owner_z(s, doc) >= z)
            merged = jnp.where(nearer, inward[s, parts[h], :], arrived[1 - side, s, parts[h], :])
            if s == 0:
                panel[s, x, parts[h], :] = merged
            else:
                ready[s, parts[h], :] = merged
                shift_copy(h, s).start()

    def spread_copy(h, s):
        part = panel.at[s, x, parts[h]]
        to = z + 1 if h < PARTS // 2 else z - 1
        return remote(part, part, spread_send.at[h, s], shift_recv.at[h, s], at_z(to))

    def spreads(h, s):
        more = z < RING - 1 if h < PARTS // 2 else z > 0
        return jnp.logical_and(takes_over[s], more)

    def ring_copies(h, s):
        part = panel.at[s, x, parts[h]]
        return (
            remote(part, part, ring_send.at[0, h, s], ring_recv.at[0, h, s], at_x(1)),
            remote(part, part, ring_send.at[1, h, s], ring_recv.at[1, h, s], at_x(-1)),
        )

    def gather(h, s):
        if s > 0:
            shift_copy(h, s).wait_recv()

            @pl.when(spreads(h, s))
            def _():
                spread_copy(h, s).start()

        for copy in ring_copies(h, s):
            copy.start()

    def pass_copy(h, s):
        forth = 1 if h < PARTS // 2 else -1
        part = panel.at[s, (x + RING - forth) % RING, parts[h]]
        return remote(part, part, pass_send.at[h, s], pass_recv.at[h, s], at_x(forth))

    def ring_pass(h, s):
        for copy in ring_copies(h, s):
            copy.wait_recv()
        pass_copy(h, s).start()

    def tile_rows_of(s, t):
        return jnp.concatenate(
            [panel[s, t, pl.ds(c * TILE, TILE), :] for c in range(lanes)], axis=1
        )

    def update(s):
        for h in range(PARTS):
            pass_copy(h, s).wait_recv()
        high, low = split(trained[...])
        count = counts[s, block % TILE]
        grad = None
        for pair in range(RING // 2):
            tiles = (2 * pair, 2 * pair + 1)
            rows = jnp.concatenate([tile_rows_of(s, t) for t in tiles], axis=0)
            contract = (((1,), (1,)), ((), ()))
            scores = (
                lax.dot_general(high, rows, contract, preferred_element_type=jnp.float32)
                + lax.dot_general(low, rows, contract, preferred_element_type=jnp.float32)
            ) * scale
            keys, lives = [], []
            for t in tiles:
                group = panel[s, t, pl.ds(code_rows, picks), :].astype(jnp.float32)
                label = panel[s, t, pl.ds(code_rows + picks, picks), :].astype(jnp.float32)
                wanted = (s * RING * RING + lab).astype(jnp.float32)
                keys.append(jnp.where(group == wanted, label, -1.0))
                live = jnp.float32(0.0)
                for k in range(RING):
                    met = jnp.logical_and(count > k, shortlist[s, k, block % TILE] == t)
                    live = jnp.where(met, jnp.float32(1.0), live)
                lives.append(jnp.full((1, TILE), live, jnp.float32))
            keys = jnp.concatenate(keys, axis=1)
            lives = jnp.concatenate(lives, axis=1)
            names = lax.broadcasted_iota(jnp.int32, scores.shape, 0).astype(jnp.float32)
            hit = names == keys[0:1, :]
            for p in range(1, picks):
                hit = jnp.logical_or(hit, names == keys[p : p + 1, :])
            resid = (jax.nn.sigmoid(scores) - jnp.where(hit, 1.0, 0.0)) * lives
            rhigh, rlow = split(resid)
            part = jnp.dot(rhigh, rows, preferred_element_type=jnp.float32) + jnp.dot(
                rlow, rows, preferred_element_type=jnp.float32
            )
            grad = part if grad is None else grad + part
        pulled = jnp.dot(pull[...], high, preferred_element_type=jnp.float32) + jnp.dot(
            pull[...], low, preferred_element_type=jnp.float32
        )
        moment = beta_rate * momentum[...] + (grad * scale + pull_rate * pulled)
        momentum[...] = moment
        trained[...] = trained[...] - learning_rate * moment

    row_start(0)

    loads[5].wait()
    ids = lax.broadcasted_iota(jnp.int32, (labels, TILE), 0)
    columns = []
    for c in range(labels // TILE):
        parent = par[pl.ds((block % 4) * (labels // TILE) + c, 1), :]
        own = lax.broadcasted_iota(jnp.int32, (labels, TILE), 1) + c * TILE
        columns.append((ids == own).astype(jnp.float32) - (ids == parent).astype(jnp.float32))
    pull[...] = jnp.transpose(jnp.concatenate(columns, axis=1)).astype(jnp.bfloat16)
    momentum[...] = jnp.zeros_like(momentum)
    for load in (loads[2], loads[3], loads[4], loads[6]):
        load.wait()

    row_wait(0)
    row_start(1)
    for s in range(STEPS):
        flow_in(0, s)
    flow_out(0, 0)
    row_wait(1)
    order = [(h, s) for h in range(PARTS) for s in range(STEPS)]
    for i in range(1, len(order)):
        if i <= STEPS:
            flow_in(1, i - 1)
        flow_out(*order[i])
        gather(*order[i - 1])
        if i >= 2:
            ring_pass(*order[i - 2])
    update(0)
    gather(*order[-1])
    ring_pass(*order[-2])
    update(1)
    ring_pass(*order[-1])
    update(2)
    update(3)

    for h in range(PARTS):
        for copy in row_copies(h):
            copy.wait_send()
        for s in range(STEPS):

            @pl.when(goes_in(h, s))
            def _():
                line_in(h, s).wait_send()

            @pl.when(jnp.logical_and(goes_out(h, s), has_near))
            def _():
                line_out(h, s, near).wait_send()

            if s > 0:
                ends = jnp.logical_and(side != h, jnp.logical_not(has_near))

                @pl.when(jnp.logical_or(jnp.logical_not(sends_over[s]), ends))
                def _():
                    shift_copy(h, s).wait_send()

                @pl.when(spreads(h, s))
                def _():
                    spread_copy(h, s).wait_send()

            for copy in ring_copies(h, s):
                copy.wait_send()
            pass_copy(h, s).wait_send()


def local(doc_count, embeddings, positives, weights, parents, owners, shortlist, counts):
    rows, width = embeddings.shape
    labels = weights.shape[0]
    picks = positives.shape[1]
    slots = shortlist.shape[2]
    tile = (width + 2 * picks, TILE)
    half = jnp.bfloat16
    dma = pltpu.SemaphoreType.DMA
    out = jax.ShapeDtypeStruct(weights.shape, jnp.float32)
    hbm = pl.BlockSpec(memory_space=pltpu.HBM)
    vmem = pl.BlockSpec(memory_space=pltpu.VMEM)
    return pl.pallas_call(
        functools.partial(train_kernel, doc_count),
        out_shape=(out, out),
        in_specs=[hbm] * 7,
        out_specs=(vmem, vmem),
        scratch_shapes=[
            pltpu.SMEM(owners.shape, jnp.int32),
            pltpu.SMEM((STEPS, TILE), jnp.int32),
            pltpu.SMEM((STEPS, slots, TILE), jnp.int32),
            pltpu.VMEM((rows, width), half),
            pltpu.VMEM((picks, rows), jnp.int32),
            pltpu.VMEM((8, TILE), jnp.int32),
            pltpu.VMEM((labels, labels), half),
            pltpu.VMEM((RING,) + tile, half),
            pltpu.VMEM((RING, tile[0] // PARTS, TILE), half),
            pltpu.VMEM((RING, tile[0] // PARTS, TILE), half),
            pltpu.VMEM((STEPS,) + tile, half),
            pltpu.VMEM((STEPS,) + tile, half),
            pltpu.VMEM((STEPS,) + tile, half),
            pltpu.VMEM((2, STEPS) + tile, half),
            pltpu.VMEM((STEPS,) + tile, half),
            pltpu.VMEM((STEPS, RING) + tile, half),
            dma((7,)),
            dma((PARTS, RING - 1)),
            dma((PARTS, RING - 1)),
            dma((PARTS, STEPS)),
            dma((PARTS, STEPS)),
            dma((2, PARTS, STEPS)),
            dma((PARTS, STEPS)),
            dma((PARTS, STEPS)),
            dma((PARTS, STEPS)),
            dma((2, PARTS, STEPS)),
            dma((2, PARTS, STEPS)),
            dma((PARTS, STEPS)),
            dma((PARTS, STEPS)),
        ],
        compiler_params=pltpu.CompilerParams(
            collective_id=0, has_side_effects=True, vmem_limit_bytes=48 * 1024 * 1024
        ),
    )(
        *(
            pltpu.with_memory_space_constraint(value, pltpu.HBM)
            for value in (
                owners,
                counts,
                jnp.transpose(shortlist, (0, 2, 1)),
                parents.reshape(-1, TILE),
                embeddings,
                positives.T,
                weights,
            )
        )
    )


def solution(mesh):
    return jax.shard_map(
        functools.partial(local, mesh.shape["doc"]),
        mesh=mesh,
        in_specs=(
            P(("doc", "lab"), None),
            P(("doc", "lab"), None),
            P(("doc", "lab"), None),
            P(),
            P(),
            P(),
            P(),
        ),
        out_specs=(P(("doc", "lab"), None), P(("doc", "lab"), None)),
        check_vma=False,
    )
```

time: 114 us -> 114 us (level)
  local copies, waits for them, and re-layouts: 7.95 us -> 1.76 us
  Pallas kernels: 105 us -> 111 us
    unnamed x16 -> x2, local copies, waits for them, and re-layouts: 7.95 us -> 1.76 us
    pallas_call x1, Pallas kernels: 105 us -> 111 us  [local(): pl.pallas_call(functools.partial(train_kernel, doc_count), out_shape=(out...]
where the time goes in v2:
time: 114 us
  Pallas kernels  111 us (97%)
  local copies, waits for them, and re-layouts  1.76 us (2%)
    pallas_call x1, Pallas kernels, local(): pl.pallas_call(functools.partial(train_kernel, doc_count), out_shape=(out...  111 us

profile of v2, /device:TPU:56, one launch (start us, length us, event | category | flops | bytes accessed | tf_op | source)
XLA Modules:
  0.0 113.7 jit_solution(5419709218114279734)
XLA Ops:
  0.6 111.3 %shard_map.86 = (f32[256,768]{1,0:T(8,128)S(1)}, f32[256,768]{1,0:T(8,128)S(1)}) custom-call(s32[4,32]{1,0:T(4,128)} %owners_all.1, s32[4,512]{1,0:T(4,128)} %counts_all.1, s32[4,4,512]{2,1,0:T(4,128)} %bitcast.4, s32[1024,128]{1,0:T(8,128)} %bitcast.3, bf16[512,768]{1,0:T(8,128)(2,1)} %embeddings.1, s32[16,512]{1,0:T(8,128)} %bitcast.5, f32[256,768]{1,0:T(8,128)} %weights.1), custom_call_target="tpu_custom_call" | custom-call | tf_op jit(solution)/shard_map/pallas_call | solution.py:422
  111.9 0.9 copy.11
  112.8 0.9 copy.12

commit v3 on v2

--- a/solution.py
+++ b/solution.py
@@ -13,6 +13,7 @@
 STEPS = 4
 RING = 4
 PARTS = 2
+OUT_LAG, GATHER_LAG, PASS_LAG = 2, 1, 1
 
 learning_rate = 0.1
 beta_rate = 0.9
@@ -91,6 +92,9 @@
         to_z = jnp.where(crosses, RING - 1 - z, z)
         return ((doc + k) % doc_count, to_z * RING + x)
 
+    def beside(k):
+        return ((doc + k) % doc_count, (z + 1 - 2 * (z % 2)) * RING + x)
+
     sends_over = [place < s for s in range(STEPS)]
     takes_over = [place + s >= span for s in range(STEPS)]
 
@@ -125,6 +129,20 @@
     def _():
         pl.semaphore_signal(barrier, inc=1, device_id=at_z(near), device_id_type=MESH)
 
+    expected = len(partners) + jnp.where(has_near, 1, 0)
+    for s in range(1, STEPS):
+        gives = jnp.logical_and(sends_over[s], jnp.logical_not(has_near))
+        gets = jnp.logical_and(takes_over[s], has_near)
+        expected += jnp.where(gives, 1, 0) + jnp.where(gets, 1, 0)
+
+        @pl.when(gives)
+        def _():
+            pl.semaphore_signal(barrier, inc=1, device_id=beside(-s), device_id_type=MESH)
+
+        @pl.when(gets)
+        def _():
+            pl.semaphore_signal(barrier, inc=1, device_id=beside(s), device_id_type=MESH)
+
     loads[0].wait()
     loads[1].wait()
     for t in range(RING):
@@ -136,7 +154,7 @@
     for h in range(PARTS):
         row[h][x] = src[x, pl.ds(h * part_rows, part_rows), :]
 
-    pl.semaphore_wait(barrier, len(partners) + jnp.where(has_near, 1, 0))
+    pl.semaphore_wait(barrier, expected)
 
     def remote(source, target, send, recv, device):
         return pltpu.make_async_remote_copy(
@@ -197,10 +215,12 @@
     def goes_out(h, s):
         return jnp.logical_or(jnp.logical_not(sends_over[s]), side != h)
 
-    def over_copy(h, s):
+    def over_copies(h, s):
+        part = outward.at[s, parts[h]]
         target = panel.at[s, x, parts[h]]
-        return remote(
-            outward.at[s, parts[h]], target, shift_send.at[h, s], shift_recv.at[h, s], across(-s, True)
+        return (
+            remote(part, target, spread_send.at[h, s], shift_recv.at[h, s], beside(-s)),
+            remote(part, target, shift_send.at[h, s], shift_recv.at[h, s], across(-s, True)),
         )
 
     def shift_copy(h, s):
@@ -209,22 +229,22 @@
             ready.at[s, parts[h]], target, shift_send.at[h, s], shift_recv.at[h, s], across(-s, False)
         )
 
-    def flow_in(h, s):
-        cand[s, parts[h], :] = row[h][owners[s, doc] % RING]
-
-        @pl.when(goes_in(h, s))
-        def _():
-            @pl.when(has_near)
-            def _():
-                line_in(h, s).wait_recv()
-                inward[s, parts[h], :] = jnp.where(
-                    owner_z(s, doc) == z, cand[s, parts[h], :], arrived[side, s, parts[h], :]
-                )
-
-            @pl.when(jnp.logical_not(has_near))
+    def flow_start(h):
+        for s in range(STEPS):
+            cand[s, parts[h], :] = row[h][owners[s, doc] % RING]
+
+            @pl.when(jnp.logical_and(goes_in(h, s), jnp.logical_not(has_near)))
             def _():
                 inward[s, parts[h], :] = cand[s, parts[h], :]
-
+                line_in(h, s).start()
+
+    def flow_in(h, s):
+        @pl.when(jnp.logical_and(goes_in(h, s), has_near))
+        def _():
+            line_in(h, s).wait_recv()
+            inward[s, parts[h], :] = jnp.where(
+                owner_z(s, doc) == z, cand[s, parts[h], :], arrived[side, s, parts[h], :]
+            )
             line_in(h, s).start()
 
     def flow_out(h, s):
@@ -245,7 +265,8 @@
 
         @pl.when(jnp.logical_and(over, jnp.logical_not(has_near)))
         def _():
-            over_copy(h, s).start()
+            for copy in over_copies(h, s):
+                copy.start()
 
         @pl.when(jnp.logical_not(sends_over[s]))
         def _():
@@ -263,8 +284,8 @@
         return remote(part, part, spread_send.at[h, s], shift_recv.at[h, s], at_z(to))
 
     def spreads(h, s):
-        more = z < RING - 1 if h < PARTS // 2 else z > 0
-        return jnp.logical_and(takes_over[s], more)
+        passes = z % 2 == (0 if h < PARTS // 2 else 1)
+        return jnp.logical_and(takes_over[s], passes)
 
     def ring_copies(h, s):
         part = panel.at[s, x, parts[h]]
@@ -359,23 +380,49 @@
 
     row_wait(0)
     row_start(1)
-    for s in range(STEPS):
-        flow_in(0, s)
-    flow_out(0, 0)
-    row_wait(1)
+    flow_start(0)
     order = [(h, s) for h in range(PARTS) for s in range(STEPS)]
-    for i in range(1, len(order)):
-        if i <= STEPS:
-            flow_in(1, i - 1)
-        flow_out(*order[i])
-        gather(*order[i - 1])
-        if i >= 2:
-            ring_pass(*order[i - 2])
-    update(0)
-    gather(*order[-1])
-    ring_pass(*order[-2])
+    units = len(order)
+
+    def when_near(act, h, s):
+        if s == 0:
+            act(h, s)
+        else:
+
+            @pl.when(jnp.logical_not(takes_over[s]))
+            def _():
+                act(h, s)
+
+    def when_over(act, h, s):
+        @pl.when(takes_over[s])
+        def _():
+            act(h, s)
+
+    for i in range(units + OUT_LAG + GATHER_LAG + PASS_LAG):
+        if i == STEPS - 1:
+            row_wait(1)
+            flow_start(1)
+        if i < units:
+            flow_in(*order[i])
+        i -= OUT_LAG
+        if 0 <= i < units:
+            flow_out(*order[i])
+        i -= GATHER_LAG
+        if 0 <= i < units:
+            when_near(gather, *order[i])
+        i -= PASS_LAG
+        if 0 <= i < units:
+            when_near(ring_pass, *order[i])
+        if i == STEPS + 1:
+            update(0)
+
+    late = [(h, s) for h, s in order if s > 0]
+    for i, unit in enumerate(late):
+        when_over(gather, *unit)
+        if i > 0:
+            when_over(ring_pass, *late[i - 1])
     update(1)
-    ring_pass(*order[-1])
+    when_over(ring_pass, *late[-1])
     update(2)
     update(3)
 
@@ -399,7 +446,7 @@
                 def _():
                     shift_copy(h, s).wait_send()
 
-                @pl.when(spreads(h, s))
+                @pl.when(jnp.logical_or(spreads(h, s), jnp.logical_and(sends_over[s], ends)))
                 def _():
                     spread_copy(h, s).wait_send()
 

time: 114 us -> 92 us (0.81)
  Pallas kernels: 111 us -> 89.4 us
    pallas_call x1, Pallas kernels: 111 us -> 89.4 us  [local(): pl.pallas_call(functools.partial(train_kernel, doc_count), out_shape=(out...]
where the time goes in v3:
time: 92 us; the launch traced here: 91.8 us
  Pallas kernels  89.4 us (97%)
  local copies, waits for them, and re-layouts  1.76 us (2%)
    pallas_call x1, Pallas kernels, local(): pl.pallas_call(functools.partial(train_kernel, doc_count), out_shape=(out...  89.4 us

profile of v3, /device:TPU:56, one launch (start us, length us, event | category | flops | bytes accessed | tf_op | source)
XLA Modules:
  0.0 91.8 jit_solution(1541259158293501790)
XLA Ops:
  0.6 89.4 %shard_map.86 = (f32[256,768]{1,0:T(8,128)S(1)}, f32[256,768]{1,0:T(8,128)S(1)}) custom-call(s32[4,32]{1,0:T(4,128)} %owners_all.1, s32[4,512]{1,0:T(4,128)} %counts_all.1, s32[4,4,512]{2,1,0:T(4,128)} %bitcast.4, s32[1024,128]{1,0:T(8,128)} %bitcast.3, bf16[512,768]{1,0:T(8,128)(2,1)} %embeddings.1, s32[16,512]{1,0:T(8,128)} %bitcast.5, f32[256,768]{1,0:T(8,128)} %weights.1), custom_call_target="tpu_custom_call" | custom-call | tf_op jit(solution)/shard_map/pallas_call | solution.py:469
  90.1 0.9 copy.11
  91.0 0.9 copy.12

commit v4 on v2

--- a/solution.py
+++ b/solution.py
@@ -12,7 +12,8 @@
 TILE = 128
 STEPS = 4
 RING = 4
-PARTS = 2
+PARTS = 4
+OUT_LAG, GATHER_LAG, PASS_LAG, UPDATE_LAG = 3, 2, 1, 2
 
 learning_rate = 0.1
 beta_rate = 0.9
@@ -23,6 +24,10 @@
     high = value.astype(jnp.bfloat16)
     low = (value - high.astype(jnp.float32)).astype(jnp.bfloat16)
     return high, low
+
+
+def part_bounds(rows):
+    return [rows // 16 * i // PARTS * 16 for i in range(PARTS + 1)]
 
 
 def train_kernel(
@@ -44,8 +49,10 @@
     par,
     pull,
     src,
-    row_first,
-    row_second,
+    row_0,
+    row_1,
+    row_2,
+    row_3,
     cand,
     inward,
     outward,
@@ -60,7 +67,6 @@
     line_recv,
     shift_send,
     shift_recv,
-    spread_send,
     ring_send,
     ring_recv,
     pass_send,
@@ -73,11 +79,12 @@
     width = embeddings.shape[1]
     lanes = width // TILE
     code_rows = lanes * TILE
-    part_rows = src.shape[1] // PARTS
+    bounds = part_bounds(src.shape[1])
+    parts = [pl.ds(a, b - a) for a, b in zip(bounds, bounds[1:])]
     picks = positives.shape[0]
     labels = weights.shape[0]
     scale = 1.0 / (float(width) ** 0.5)
-    row = (row_first, row_second)
+    row = (row_0, row_1, row_2, row_3)
     span = doc_count // 2
     place = doc % span
 
@@ -134,7 +141,7 @@
         src[t, pl.ds(code_rows, picks), :] = (code // labels).astype(jnp.float32).astype(jnp.bfloat16)
         src[t, pl.ds(code_rows + picks, picks), :] = (code % labels).astype(jnp.float32).astype(jnp.bfloat16)
     for h in range(PARTS):
-        row[h][x] = src[x, pl.ds(h * part_rows, part_rows), :]
+        row[h][x] = src[x, parts[h], :]
 
     pl.semaphore_wait(barrier, len(partners) + jnp.where(has_near, 1, 0))
 
@@ -147,8 +154,6 @@
             device_id=device,
             device_id_type=MESH,
         )
-
-    parts = [pl.ds(h * part_rows, part_rows) for h in range(PARTS)]
 
     def row_copies(h):
         return [
@@ -191,80 +196,51 @@
             at_z(to),
         )
 
-    def goes_in(h, s):
-        return jnp.logical_or(jnp.logical_not(sends_over[s]), side == h)
-
-    def goes_out(h, s):
-        return jnp.logical_or(jnp.logical_not(sends_over[s]), side != h)
-
-    def over_copy(h, s):
-        target = panel.at[s, x, parts[h]]
-        return remote(
-            outward.at[s, parts[h]], target, shift_send.at[h, s], shift_recv.at[h, s], across(-s, True)
-        )
-
     def shift_copy(h, s):
         target = panel.at[s, x, parts[h]]
         return remote(
-            ready.at[s, parts[h]], target, shift_send.at[h, s], shift_recv.at[h, s], across(-s, False)
-        )
-
-    def flow_in(h, s):
-        cand[s, parts[h], :] = row[h][owners[s, doc] % RING]
-
-        @pl.when(goes_in(h, s))
-        def _():
-            @pl.when(has_near)
-            def _():
-                line_in(h, s).wait_recv()
-                inward[s, parts[h], :] = jnp.where(
-                    owner_z(s, doc) == z, cand[s, parts[h], :], arrived[side, s, parts[h], :]
-                )
+            ready.at[s, parts[h]],
+            target,
+            shift_send.at[h, s],
+            shift_recv.at[h, s],
+            across(-s, sends_over[s]),
+        )
+
+    def flow_start(h):
+        for s in range(STEPS):
+            cand[s, parts[h], :] = row[h][owners[s, doc] % RING]
 
             @pl.when(jnp.logical_not(has_near))
             def _():
                 inward[s, parts[h], :] = cand[s, parts[h], :]
-
+                line_in(h, s).start()
+
+    def flow_in(h, s):
+        @pl.when(has_near)
+        def _():
+            line_in(h, s).wait_recv()
+            inward[s, parts[h], :] = jnp.where(
+                owner_z(s, doc) == z, cand[s, parts[h], :], arrived[side, s, parts[h], :]
+            )
             line_in(h, s).start()
 
     def flow_out(h, s):
-        mine = owner_z(s, doc) == z
-
-        @pl.when(goes_out(h, s))
+        line_out(h, s, far).wait_recv()
+
+        @pl.when(has_near)
         def _():
-            line_out(h, s, far).wait_recv()
             outward[s, parts[h], :] = jnp.where(
-                mine, cand[s, parts[h], :], arrived[1 - side, s, parts[h], :]
+                owner_z(s, doc) == z, cand[s, parts[h], :], arrived[1 - side, s, parts[h], :]
             )
-
-            @pl.when(has_near)
-            def _():
-                line_out(h, s, near).start()
-
-        over = jnp.logical_and(sends_over[s], side != h)
-
-        @pl.when(jnp.logical_and(over, jnp.logical_not(has_near)))
-        def _():
-            over_copy(h, s).start()
-
-        @pl.when(jnp.logical_not(sends_over[s]))
-        def _():
-            nearer = jnp.where(low_half, owner_z(s, doc) <= z, owner_z(s, doc) >= z)
-            merged = jnp.where(nearer, inward[s, parts[h], :], arrived[1 - side, s, parts[h], :])
-            if s == 0:
-                panel[s, x, parts[h], :] = merged
-            else:
-                ready[s, parts[h], :] = merged
-                shift_copy(h, s).start()
-
-    def spread_copy(h, s):
-        part = panel.at[s, x, parts[h]]
-        to = z + 1 if h < PARTS // 2 else z - 1
-        return remote(part, part, spread_send.at[h, s], shift_recv.at[h, s], at_z(to))
-
-    def spreads(h, s):
-        more = z < RING - 1 if h < PARTS // 2 else z > 0
-        return jnp.logical_and(takes_over[s], more)
+            line_out(h, s, near).start()
+
+        nearer = jnp.where(low_half, owner_z(s, doc) <= z, owner_z(s, doc) >= z)
+        merged = jnp.where(nearer, inward[s, parts[h], :], arrived[1 - side, s, parts[h], :])
+        if s == 0:
+            panel[s, x, parts[h], :] = merged
+        else:
+            ready[s, parts[h], :] = merged
+            shift_copy(h, s).start()
 
     def ring_copies(h, s):
         part = panel.at[s, x, parts[h]]
@@ -277,15 +253,11 @@
         if s > 0:
             shift_copy(h, s).wait_recv()
 
-            @pl.when(spreads(h, s))
-            def _():
-                spread_copy(h, s).start()
-
         for copy in ring_copies(h, s):
             copy.start()
 
     def pass_copy(h, s):
-        forth = 1 if h < PARTS // 2 else -1
+        forth = 1 if h % 2 == 0 else -1
         part = panel.at[s, (x + RING - forth) % RING, parts[h]]
         return remote(part, part, pass_send.at[h, s], pass_recv.at[h, s], at_x(forth))
 
@@ -359,50 +331,44 @@
 
     row_wait(0)
     row_start(1)
-    for s in range(STEPS):
-        flow_in(0, s)
-    flow_out(0, 0)
-    row_wait(1)
+    flow_start(0)
     order = [(h, s) for h in range(PARTS) for s in range(STEPS)]
-    for i in range(1, len(order)):
-        if i <= STEPS:
-            flow_in(1, i - 1)
-        flow_out(*order[i])
-        gather(*order[i - 1])
-        if i >= 2:
-            ring_pass(*order[i - 2])
-    update(0)
-    gather(*order[-1])
-    ring_pass(*order[-2])
-    update(1)
-    ring_pass(*order[-1])
-    update(2)
-    update(3)
+    units = len(order)
+    for i in range(units + OUT_LAG + GATHER_LAG + PASS_LAG + UPDATE_LAG):
+        h = (i + 2) // STEPS
+        if (i + 2) % STEPS == 0 and h < PARTS:
+            row_wait(h)
+            if h + 1 < PARTS:
+                row_start(h + 1)
+            flow_start(h)
+        if i < units:
+            flow_in(*order[i])
+        i -= OUT_LAG
+        if 0 <= i < units:
+            flow_out(*order[i])
+        i -= GATHER_LAG
+        if 0 <= i < units:
+            gather(*order[i])
+        i -= PASS_LAG
+        if 0 <= i < units:
+            ring_pass(*order[i])
+        i -= UPDATE_LAG
+        if i >= units - STEPS:
+            update(i + STEPS - units)
 
     for h in range(PARTS):
         for copy in row_copies(h):
             copy.wait_send()
         for s in range(STEPS):
 
-            @pl.when(goes_in(h, s))
-            def _():
-                line_in(h, s).wait_send()
-
-            @pl.when(jnp.logical_and(goes_out(h, s), has_near))
+            line_in(h, s).wait_send()
+
+            @pl.when(has_near)
             def _():
                 line_out(h, s, near).wait_send()
 
             if s > 0:
-                ends = jnp.logical_and(side != h, jnp.logical_not(has_near))
-
-                @pl.when(jnp.logical_or(jnp.logical_not(sends_over[s]), ends))
-                def _():
-                    shift_copy(h, s).wait_send()
-
-                @pl.when(spreads(h, s))
-                def _():
-                    spread_copy(h, s).wait_send()
-
+                shift_copy(h, s).wait_send()
             for copy in ring_copies(h, s):
                 copy.wait_send()
             pass_copy(h, s).wait_send()
@@ -414,6 +380,7 @@
     picks = positives.shape[1]
     slots = shortlist.shape[2]
     tile = (width + 2 * picks, TILE)
+    bounds = part_bounds(tile[0])
     half = jnp.bfloat16
     dma = pltpu.SemaphoreType.DMA
     out = jax.ShapeDtypeStruct(weights.shape, jnp.float32)
@@ -433,8 +400,7 @@
             pltpu.VMEM((8, TILE), jnp.int32),
             pltpu.VMEM((labels, labels), half),
             pltpu.VMEM((RING,) + tile, half),
-            pltpu.VMEM((RING, tile[0] // PARTS, TILE), half),
-            pltpu.VMEM((RING, tile[0] // PARTS, TILE), half),
+            *[pltpu.VMEM((RING, b - a, TILE), half) for a, b in zip(bounds, bounds[1:])],
             pltpu.VMEM((STEPS,) + tile, half),
             pltpu.VMEM((STEPS,) + tile, half),
             pltpu.VMEM((STEPS,) + tile, half),
@@ -447,7 +413,6 @@
             dma((PARTS, STEPS)),
             dma((PARTS, STEPS)),
             dma((2, PARTS, STEPS)),
-            dma((PARTS, STEPS)),
             dma((PARTS, STEPS)),
             dma((PARTS, STEPS)),
             dma((2, PARTS, STEPS)),

time: 114 us -> 83.6 us (0.73)
  Pallas kernels: 111 us -> 81.1 us
    pallas_call x1, Pallas kernels: 111 us -> 81.1 us  [local(): pl.pallas_call(functools.partial(train_kernel, doc_count), out_shape=(out...]
where the time goes in v4:
time: 83.6 us; the launch traced here: 83.5 us
  Pallas kernels  81.1 us (97%)
  local copies, waits for them, and re-layouts  1.76 us (2%)
    pallas_call x1, Pallas kernels, local(): pl.pallas_call(functools.partial(train_kernel, doc_count), out_shape=(out...  81.1 us
    unnamed x2, local copies, waits for them, and re-layouts  1.76 us

profile of v4, /device:TPU:56, one launch (start us, length us, event | category | flops | bytes accessed | tf_op | source)
XLA Modules:
  0.0 83.5 jit_solution(1405488803906146547)
XLA Ops:
  0.6 81.1 %shard_map.86 = (f32[256,768]{1,0:T(8,128)S(1)}, f32[256,768]{1,0:T(8,128)S(1)}) custom-call(s32[4,32]{1,0:T(4,128)} %owners_all.1, s32[4,512]{1,0:T(4,128)} %counts_all.1, s32[4,4,512]{2,1,0:T(4,128)} %bitcast.4, s32[1024,128]{1,0:T(8,128)} %bitcast.3, bf16[512,768]{1,0:T(8,128)(2,1)} %embeddings.1, s32[16,512]{1,0:T(8,128)} %bitcast.5, f32[256,768]{1,0:T(8,128)} %weights.1), custom_call_target="tpu_custom_call" | custom-call | tf_op jit(solution)/shard_map/pallas_call | solution.py:389
  81.7 0.9 %copy.11 = f32[256,768]{1,0:T(8,128)} copy(f32[256,768]{1,0:T(8,128)S(1)} %get-tuple-element.4) | data formatting | bytes 1572864
  82.6 0.9 %copy.12 = f32[256,768]{1,0:T(8,128)} copy(f32[256,768]{1,0:T(8,128)S(1)} %get-tuple-element.5) | data formatting | bytes 1572864

commit v5 on v4

--- a/solution.py
+++ b/solution.py
@@ -12,8 +12,10 @@
 TILE = 128
 STEPS = 4
 RING = 4
-PARTS = 4
-OUT_LAG, GATHER_LAG, PASS_LAG, UPDATE_LAG = 3, 2, 1, 2
+SIZES = (6, 8, 12, 12, 12)
+PARTS = len(SIZES)
+AHEAD = 3
+OUT_LAG, GATHER_LAG, PASS_LAG, UPDATE_LAG = 3, 1, 2, 2
 
 learning_rate = 0.1
 beta_rate = 0.9
@@ -27,7 +29,7 @@
 
 
 def part_bounds(rows):
-    return [rows // 16 * i // PARTS * 16 for i in range(PARTS + 1)]
+    return [rows // sum(SIZES) * sum(SIZES[:i]) for i in range(PARTS + 1)]
 
 
 def train_kernel(
@@ -48,11 +50,14 @@
     pos,
     par,
     pull,
+    high,
+    low,
     src,
     row_0,
     row_1,
     row_2,
     row_3,
+    row_4,
     cand,
     inward,
     outward,
@@ -84,7 +89,7 @@
     picks = positives.shape[0]
     labels = weights.shape[0]
     scale = 1.0 / (float(width) ** 0.5)
-    row = (row_0, row_1, row_2, row_3)
+    row = (row_0, row_1, row_2, row_3, row_4)
     span = doc_count // 2
     place = doc % span
 
@@ -271,10 +276,19 @@
             [panel[s, t, pl.ds(c * TILE, TILE), :] for c in range(lanes)], axis=1
         )
 
+    def prepare(s):
+        whigh, wlow = split(trained[...])
+        high[...] = whigh
+        low[...] = wlow
+        pulled = pull_rate * (
+            jnp.dot(pull[...], whigh, preferred_element_type=jnp.float32)
+            + jnp.dot(pull[...], wlow, preferred_element_type=jnp.float32)
+        )
+        momentum[...] = pulled if s == 0 else beta_rate * momentum[...] + pulled
+
     def update(s):
         for h in range(PARTS):
             pass_copy(h, s).wait_recv()
-        high, low = split(trained[...])
         count = counts[s, block % TILE]
         grad = None
         for pair in range(RING // 2):
@@ -282,8 +296,8 @@
             rows = jnp.concatenate([tile_rows_of(s, t) for t in tiles], axis=0)
             contract = (((1,), (1,)), ((), ()))
             scores = (
-                lax.dot_general(high, rows, contract, preferred_element_type=jnp.float32)
-                + lax.dot_general(low, rows, contract, preferred_element_type=jnp.float32)
+                lax.dot_general(high[...], rows, contract, preferred_element_type=jnp.float32)
+                + lax.dot_general(low[...], rows, contract, preferred_element_type=jnp.float32)
             ) * scale
             keys, lives = [], []
             for t in tiles:
@@ -308,14 +322,14 @@
                 rlow, rows, preferred_element_type=jnp.float32
             )
             grad = part if grad is None else grad + part
-        pulled = jnp.dot(pull[...], high, preferred_element_type=jnp.float32) + jnp.dot(
-            pull[...], low, preferred_element_type=jnp.float32
-        )
-        moment = beta_rate * momentum[...] + (grad * scale + pull_rate * pulled)
+        moment = momentum[...] + grad * scale
         momentum[...] = moment
         trained[...] = trained[...] - learning_rate * moment
-
-    row_start(0)
+        if s < STEPS - 1:
+            prepare(s + 1)
+
+    for h in range(AHEAD):
+        row_start(h)
 
     loads[5].wait()
     ids = lax.broadcasted_iota(jnp.int32, (labels, TILE), 0)
@@ -325,21 +339,21 @@
         own = lax.broadcasted_iota(jnp.int32, (labels, TILE), 1) + c * TILE
         columns.append((ids == own).astype(jnp.float32) - (ids == parent).astype(jnp.float32))
     pull[...] = jnp.transpose(jnp.concatenate(columns, axis=1)).astype(jnp.bfloat16)
-    momentum[...] = jnp.zeros_like(momentum)
     for load in (loads[2], loads[3], loads[4], loads[6]):
         load.wait()
+    prepare(0)
 
     row_wait(0)
-    row_start(1)
+    row_start(AHEAD)
     flow_start(0)
     order = [(h, s) for h in range(PARTS) for s in range(STEPS)]
     units = len(order)
     for i in range(units + OUT_LAG + GATHER_LAG + PASS_LAG + UPDATE_LAG):
-        h = (i + 2) // STEPS
-        if (i + 2) % STEPS == 0 and h < PARTS:
+        h = (i + 3) // STEPS
+        if (i + 3) % STEPS == 0 and 0 < h < PARTS:
             row_wait(h)
-            if h + 1 < PARTS:
-                row_start(h + 1)
+            if h + AHEAD < PARTS:
+                row_start(h + AHEAD)
             flow_start(h)
         if i < units:
             flow_in(*order[i])
@@ -399,6 +413,8 @@
             pltpu.VMEM((picks, rows), jnp.int32),
             pltpu.VMEM((8, TILE), jnp.int32),
             pltpu.VMEM((labels, labels), half),
+            pltpu.VMEM(weights.shape, half),
+            pltpu.VMEM(weights.shape, half),
             pltpu.VMEM((RING,) + tile, half),
             *[pltpu.VMEM((RING, b - a, TILE), half) for a, b in zip(bounds, bounds[1:])],
             pltpu.VMEM((STEPS,) + tile, half),

time: 83.6 us -> 79.7 us (0.953)
  Pallas kernels: 81.1 us -> 77.2 us
    pallas_call x1, Pallas kernels: 81.1 us -> 77.2 us  [local(): pl.pallas_call(functools.partial(train_kernel, doc_count), out_shape=(out...]
where the time goes in v5:
time: 79.7 us; the launch traced here: 79.6 us
  Pallas kernels  77.2 us (97%)
  local copies, waits for them, and re-layouts  1.76 us (2%)
    pallas_call x1, Pallas kernels, local(): pl.pallas_call(functools.partial(train_kernel, doc_count), out_shape=(out...  77.2 us
    unnamed x2, local copies, waits for them, and re-layouts  1.76 us

profile of v5, /device:TPU:56, one launch (start us, length us, event | category | flops | bytes accessed | tf_op | source)
XLA Modules:
  0.0 79.6 jit_solution(17871657162377677797)
XLA Ops:
  0.6 77.2 %shard_map.86 = (f32[256,768]{1,0:T(8,128)S(1)}, f32[256,768]{1,0:T(8,128)S(1)}) custom-call(s32[4,32]{1,0:T(4,128)} %owners_all.1, s32[4,512]{1,0:T(4,128)} %counts_all.1, s32[4,4,512]{2,1,0:T(4,128)} %bitcast.4, s32[1024,128]{1,0:T(8,128)} %bitcast.3, bf16[512,768]{1,0:T(8,128)(2,1)} %embeddings.1, s32[16,512]{1,0:T(8,128)} %bitcast.5, f32[256,768]{1,0:T(8,128)} %weights.1), custom_call_target="tpu_custom_call" | custom-call | tf_op jit(solution)/shard_map/pallas_call | solution.py:403
  77.8 0.9 %copy.11 = f32[256,768]{1,0:T(8,128)} copy(f32[256,768]{1,0:T(8,128)S(1)} %get-tuple-element.4) | data formatting | bytes 1572864
  78.7 0.9 %copy.12 = f32[256,768]{1,0:T(8,128)} copy(f32[256,768]{1,0:T(8,128)S(1)} %get-tuple-element.5) | data formatting | bytes 1572864

commit v6 on v5

--- a/solution.py
+++ b/solution.py
@@ -12,10 +12,10 @@
 TILE = 128
 STEPS = 4
 RING = 4
-SIZES = (6, 8, 12, 12, 12)
+SIZES = (8, 14, 14, 14)
 PARTS = len(SIZES)
 AHEAD = 3
-OUT_LAG, GATHER_LAG, PASS_LAG, UPDATE_LAG = 3, 1, 2, 2
+OUT_LAG, GATHER_LAG, PASS_LAG, UPDATE_LAG = 3, 2, 1, 1
 
 learning_rate = 0.1
 beta_rate = 0.9
@@ -43,6 +43,7 @@
     weights,
     trained,
     momentum,
+    last,
     owners,
     counts,
     shortlist,
@@ -57,7 +58,6 @@
     row_1,
     row_2,
     row_3,
-    row_4,
     cand,
     inward,
     outward,
@@ -89,7 +89,7 @@
     picks = positives.shape[0]
     labels = weights.shape[0]
     scale = 1.0 / (float(width) ** 0.5)
-    row = (row_0, row_1, row_2, row_3, row_4)
+    row = (row_0, row_1, row_2, row_3)
     span = doc_count // 2
     place = doc % span
 
@@ -169,7 +169,7 @@
                 row_recv.at[h, k - 1],
                 at_x(k),
             )
-            for k in range(1, RING)
+            for k in (2, 1, 3)
         ]
 
     def row_start(h):
@@ -322,11 +322,13 @@
                 rlow, rows, preferred_element_type=jnp.float32
             )
             grad = part if grad is None else grad + part
+        if s == STEPS - 1:
+            last[...] = grad * scale
+            return
         moment = momentum[...] + grad * scale
         momentum[...] = moment
         trained[...] = trained[...] - learning_rate * moment
-        if s < STEPS - 1:
-            prepare(s + 1)
+        prepare(s + 1)
 
     for h in range(AHEAD):
         row_start(h)
@@ -400,11 +402,11 @@
     out = jax.ShapeDtypeStruct(weights.shape, jnp.float32)
     hbm = pl.BlockSpec(memory_space=pltpu.HBM)
     vmem = pl.BlockSpec(memory_space=pltpu.VMEM)
-    return pl.pallas_call(
+    weight, moment, last = pl.pallas_call(
         functools.partial(train_kernel, doc_count),
-        out_shape=(out, out),
+        out_shape=(out, out, out),
         in_specs=[hbm] * 7,
-        out_specs=(vmem, vmem),
+        out_specs=(vmem, vmem, vmem),
         scratch_shapes=[
             pltpu.SMEM(owners.shape, jnp.int32),
             pltpu.SMEM((STEPS, TILE), jnp.int32),
@@ -453,6 +455,8 @@
             )
         )
     )
+    moment = moment + last
+    return weight - learning_rate * moment, moment
 
 
 def solution(mesh):

time: 79.7 us -> 79.6 us (level)
  the two profiles are of different devices: /device:TPU:56 before, /device:TPU:6 now
where the time goes in v6:
time: 79.6 us; the launch traced here: 79.5 us
  Pallas kernels  77.5 us (97%)
  other arithmetic  1.28 us (2%)
    pallas_call x1, Pallas kernels, local(): pl.pallas_call(functools.partial(train_kernel, doc_count), out_shape=(out...  77.5 us

profile of v6, /device:TPU:6, one launch (start us, length us, event | category | flops | bytes accessed | tf_op | source)
XLA Modules:
  0.0 79.5 jit_solution(13826209784851142644)
XLA Ops:
  0.6 77.5 %shard_map.86 = (f32[256,768]{1,0:T(8,128)S(1)}, f32[256,768]{1,0:T(8,128)S(1)}, f32[256,768]{1,0:T(8,128)S(1)}) custom-call(s32[4,32]{1,0:T(4,128)} %owners_all.1, s32[4,512]{1,0:T(4,128)} %counts_all.1, s32[4,4,512]{2,1,0:T(4,128)} %bitcast.4, s32[1024,128]{1,0:T(8,128)} %bitcast.3, bf16[512,768]{1,0:T(8,128)(2,1)} %embeddings.1, s32[16,512]{1,0:T(8,128)} %bitcast.5, ...), custom_call_target="tpu_custom_call" | custom-call | tf_op jit(solution)/shard_map/pallas_call | solution.py:405
  78.2 1.3 %multiply_subtract_fusion = (f32[256,768]{1,0:T(8,128)}, f32[256,768]{1,0:T(8,128)}) fusion(f32[256,768]{1,0:T(8,128)S(1)} %get-tuple-element.5, f32[256,768]{1,0:T(8,128)S(1)} %get-tuple-element.6, f32[256,768]{1,0:T(8,128)S(1)} %get-tuple-element.7), kind=kLoop, calls=%fused_computation | loop fusion | flops 589824 | bytes 3932160 | tf_op jit(solution)/shard_map/sub | solution.py:459

commit v7 on v6

--- a/solution.py
+++ b/solution.py
@@ -12,10 +12,10 @@
 TILE = 128
 STEPS = 4
 RING = 4
-SIZES = (8, 14, 14, 14)
+SIZES = (8, 10, 10, 12, 10)
 PARTS = len(SIZES)
-AHEAD = 3
-OUT_LAG, GATHER_LAG, PASS_LAG, UPDATE_LAG = 3, 2, 1, 1
+AHEAD = 5
+OUT_LAG, GATHER_LAG, PASS_LAG, UPDATE_LAG = 3, 1, 2, 2
 
 learning_rate = 0.1
 beta_rate = 0.9
@@ -58,6 +58,7 @@
     row_1,
     row_2,
     row_3,
+    row_4,
     cand,
     inward,
     outward,
@@ -89,7 +90,7 @@
     picks = positives.shape[0]
     labels = weights.shape[0]
     scale = 1.0 / (float(width) ** 0.5)
-    row = (row_0, row_1, row_2, row_3)
+    row = (row_0, row_1, row_2, row_3, row_4)
     span = doc_count // 2
     place = doc % span
 
@@ -346,7 +347,8 @@
     prepare(0)
 
     row_wait(0)
-    row_start(AHEAD)
+    if AHEAD < PARTS:
+        row_start(AHEAD)
     flow_start(0)
     order = [(h, s) for h in range(PARTS) for s in range(STEPS)]
     units = len(order)

time: 79.6 us -> 79.9 us (level)
  the two profiles are of different devices: /device:TPU:6 before, /device:TPU:56 now
where the time goes in v7:
time: 79.9 us; the launch traced here: 78.4 us
  Pallas kernels  76.5 us (96%)
  other arithmetic  1.28 us (2%)
    pallas_call x1, Pallas kernels, local(): pl.pallas_call(functools.partial(train_kernel, doc_count), out_shape=(out...  76.5 us

profile of v7, /device:TPU:56, one launch (start us, length us, event | category | flops | bytes accessed | tf_op | source)
XLA Modules:
  0.0 78.4 jit_solution(13872784993575432914)
XLA Ops:
  0.6 76.5 %shard_map.86 = (f32[256,768]{1,0:T(8,128)S(1)}, f32[256,768]{1,0:T(8,128)S(1)}, f32[256,768]{1,0:T(8,128)S(1)}) custom-call(s32[4,32]{1,0:T(4,128)} %owners_all.1, s32[4,512]{1,0:T(4,128)} %counts_all.1, s32[4,4,512]{2,1,0:T(4,128)} %bitcast.4, s32[1024,128]{1,0:T(8,128)} %bitcast.3, bf16[512,768]{1,0:T(8,128)(2,1)} %embeddings.1, s32[16,512]{1,0:T(8,128)} %bitcast.5, ...), custom_call_target="tpu_custom_call" | custom-call | tf_op jit(solution)/shard_map/pallas_call | solution.py:407
  77.1 1.3 %multiply_subtract_fusion = (f32[256,768]{1,0:T(8,128)}, f32[256,768]{1,0:T(8,128)}) fusion(f32[256,768]{1,0:T(8,128)S(1)} %get-tuple-element.5, f32[256,768]{1,0:T(8,128)S(1)} %get-tuple-element.6, f32[256,768]{1,0:T(8,128)S(1)} %get-tuple-element.7), kind=kLoop, calls=%fused_computation | loop fusion | flops 589824 | bytes 3932160 | tf_op jit(solution)/shard_map/sub | solution.py:461

commit v8 on v6

--- a/solution.py
+++ b/solution.py
@@ -12,10 +12,10 @@
 TILE = 128
 STEPS = 4
 RING = 4
-SIZES = (8, 14, 14, 14)
+SIZES = (7, 12, 16, 15)
 PARTS = len(SIZES)
-AHEAD = 3
-OUT_LAG, GATHER_LAG, PASS_LAG, UPDATE_LAG = 3, 2, 1, 1
+AHEAD = 4
+OUT_LAG, GATHER_LAG, PASS_LAG, UPDATE_LAG = 2, 2, 1, 2
 
 learning_rate = 0.1
 beta_rate = 0.9
@@ -346,13 +346,12 @@
     prepare(0)
 
     row_wait(0)
-    row_start(AHEAD)
     flow_start(0)
     order = [(h, s) for h in range(PARTS) for s in range(STEPS)]
     units = len(order)
     for i in range(units + OUT_LAG + GATHER_LAG + PASS_LAG + UPDATE_LAG):
-        h = (i + 3) // STEPS
-        if (i + 3) % STEPS == 0 and 0 < h < PARTS:
+        h = i // STEPS + 1
+        if i % STEPS == 0 and h < PARTS:
             row_wait(h)
             if h + AHEAD < PARTS:
                 row_start(h + AHEAD)

time: 79.6 us -> 79.4 us (level)
  no operation moved by 1% of the time
where the time goes in v8:
time: 79.4 us; the launch traced here: 79.2 us
  Pallas kernels  77.3 us (97%)
  other arithmetic  1.28 us (2%)
    pallas_call x1, Pallas kernels, local(): pl.pallas_call(functools.partial(train_kernel, doc_count), out_shape=(out...  77.3 us

profile of v8, /device:TPU:6, one launch (start us, length us, event | category | flops | bytes accessed | tf_op | source)
XLA Modules:
  0.0 79.2 jit_solution(11561966708604905475)
XLA Ops:
  0.6 77.3 %shard_map.86 = (f32[256,768]{1,0:T(8,128)S(1)}, f32[256,768]{1,0:T(8,128)S(1)}, f32[256,768]{1,0:T(8,128)S(1)}) custom-call(s32[4,32]{1,0:T(4,128)} %owners_all.1, s32[4,512]{1,0:T(4,128)} %counts_all.1, s32[4,4,512]{2,1,0:T(4,128)} %bitcast.4, s32[1024,128]{1,0:T(8,128)} %bitcast.3, bf16[512,768]{1,0:T(8,128)(2,1)} %embeddings.1, s32[16,512]{1,0:T(8,128)} %bitcast.5, ...), custom_call_target="tpu_custom_call" | custom-call | tf_op jit(solution)/shard_map/pallas_call | solution.py:404
  77.9 1.3 %multiply_subtract_fusion = (f32[256,768]{1,0:T(8,128)}, f32[256,768]{1,0:T(8,128)}) fusion(f32[256,768]{1,0:T(8,128)S(1)} %get-tuple-element.5, f32[256,768]{1,0:T(8,128)S(1)} %get-tuple-element.6, f32[256,768]{1,0:T(8,128)S(1)} %get-tuple-element.7), kind=kLoop, calls=%fused_computation | loop fusion | flops 589824 | bytes 3932160 | tf_op jit(solution)/shard_map/sub | solution.py:458
